TPU v7x, 32 devices: a whole 2x2x4 slice. The times are simulated.
32 devices in a mesh: seq: 16 (over z, y, x), head: 2 (over core).
Axes of the slice: x: 2, y: 2, z: 4, core: 2. Of those that a mesh axis runs over, the one named last changes fastest.
Arguments:
- queries: bfloat16 [4096, 768], P('seq', 'head'), may hold values from -160 to 160
- keys: bfloat16 [4096, 768], P('seq', 'head'), may hold values from -40 to 40
- values: bfloat16 [4096, 768], P('seq', 'head'), may hold values from -6 to 6
- token_perm: int32 [6, 4096], P('head'), may hold values from 0 to 4095, as said below
- pair_blocks: int32 [6, 64, 4], P('head', 'seq'), may hold values from 0 to 63, as said below
- pair_counts: int32 [6, 64], P('head', 'seq'), may hold values from 2 to 4
- out_weight: bfloat16 [768, 5120], P('head'), may hold values from -0.875 to 0.875
Outputs:
- layer_out: bfloat16 [4096, 5120], P('seq', 'head')
Inputs may be any that keep to these rules, and one draw needn't show every extreme that they name: Each row token_perm[h] is a permutation of the tokens 0 to 4095; position p belongs to index p // 256 of seq. Of the tokens of one index of seq, at most 32 take positions of any one index, for every head. pair_blocks[h, b, r] is a key block of head h for query block b; the 4 entries of one list are distinct. Block c belongs to index c // 4 of seq. All entries, live or not, of the 4 query blocks of one index of seq name at most one block of any other index and none of their own. The first pair_counts[h, b] entries of pair_blocks[h, b] are live; the others are not visible.
All inputs are finite; a program needn't handle non-finite values.
Results may differ from a plain program's by a relative error of at most 0.013.
Values may be sent and summed in bfloat16 or wider, within the bound.
A program may use at most 64 MiB of HBM per device.

v0:
```python
import math

import jax
import jax.numpy as jnp
from jax import lax
from jax.sharding import PartitionSpec as P

HEAD_SIZE = 128
BLOCKS_DEV = 4


def body(queries, keys, values, token_perm, pair_blocks, pair_counts, out_weight):
    tok_rows = queries.shape[0]
    heads_here = token_perm.shape[0]
    list_len = pair_blocks.shape[2]
    seq_count = lax.axis_size("seq")
    lot_size = 2 * tok_rows // seq_count
    block_rows = tok_rows // BLOCKS_DEV
    myself = lax.axis_index("seq")
    by_owner = token_perm.reshape(heads_here, seq_count, tok_rows)
    from_here = by_owner // tok_rows == myself
    lot_rank = jnp.cumsum(from_here.astype(jnp.int32), axis=2) - 1
    slot_hit = from_here[..., None] & (lot_rank[..., None] == jnp.arange(lot_size, dtype=jnp.int32))
    local_row = by_owner - myself * tok_rows
    send_row = jnp.sum(jnp.where(slot_hit, local_row[..., None], 0), axis=2)
    send_live = jnp.any(slot_hit, axis=2)
    held_tokens = lax.dynamic_slice_in_dim(token_perm, myself * tok_rows, tok_rows, axis=1)
    held_source = held_tokens // tok_rows
    source_hot = (held_source[..., None] == jnp.arange(seq_count, dtype=jnp.int32)).astype(
        jnp.int32
    )
    held_rank = jnp.sum(jnp.cumsum(source_hot, axis=1) * source_hot, axis=2) - 1
    held_flat = held_source * lot_size + held_rank
    stacked = jnp.concatenate(
        [
            queries.reshape(tok_rows, heads_here, HEAD_SIZE),
            keys.reshape(tok_rows, heads_here, HEAD_SIZE),
            values.reshape(tok_rows, heads_here, HEAD_SIZE),
        ],
        axis=2,
    ).transpose(1, 0, 2)
    outgoing = jax.vmap(lambda table, picks: table[picks])(
        stacked, send_row.reshape(heads_here, -1)
    )
    outgoing = outgoing.reshape(heads_here, seq_count, lot_size, 3 * HEAD_SIZE)
    logit_scale_factor = 1.0 / math.sqrt(HEAD_SIZE)
    arrived = lax.all_to_all(outgoing, "seq", split_axis=1, concat_axis=1, tiled=True)
    head_count = arrived.shape[0]
    arrived_flat = arrived.reshape(head_count, seq_count * lot_size, 3 * HEAD_SIZE)
    grouped = jax.vmap(lambda table, picks: table[picks])(arrived_flat, held_flat)
    query_own = grouped[..., :HEAD_SIZE]
    key_own = grouped[..., HEAD_SIZE : 2 * HEAD_SIZE]
    value_own = grouped[..., 2 * HEAD_SIZE :]
    blocks_flat = grouped[..., HEAD_SIZE:].reshape(
        head_count * BLOCKS_DEV, block_rows, 2 * HEAD_SIZE
    )
    owners = pair_blocks // BLOCKS_DEV
    head_ids = jnp.arange(head_count, dtype=jnp.int32)
    block_code = pair_blocks % BLOCKS_DEV + BLOCKS_DEV * head_ids[:, None, None]
    owner_hit = owners.reshape(head_count, -1)[:, :, None] == jnp.arange(seq_count, dtype=jnp.int32)
    wanted = jnp.max(
        jnp.where(owner_hit, block_code.reshape(head_count, -1)[:, :, None], 0), axis=1
    )
    fetched = lax.all_to_all(
        blocks_flat[lax.all_to_all(wanted.T, "seq", split_axis=0, concat_axis=0, tiled=True)],
        "seq",
        split_axis=0,
        concat_axis=0,
        tiled=True,
    )
    far_rows = fetched[owners, head_ids[:, None, None]]
    near_scores = (
        jnp.einsum("hqd,hkd->hqk", query_own, key_own, preferred_element_type=jnp.float32)
        * logit_scale_factor
    )
    query_blocks = query_own.reshape(head_count, BLOCKS_DEV, block_rows, HEAD_SIZE)
    distant_scores = (
        jnp.einsum(
            "hbqd,hbrkd->hbqrk",
            query_blocks,
            far_rows[..., :HEAD_SIZE],
            preferred_element_type=jnp.float32,
        )
        * logit_scale_factor
    )
    live_mask = jnp.arange(list_len, dtype=jnp.int32) < pair_counts[..., None]
    distant_scores = jnp.where(live_mask[:, :, None, :, None], distant_scores, -jnp.inf)
    distant_scores = distant_scores.reshape(head_count, tok_rows, list_len * block_rows)
    row_max = jnp.maximum(jnp.max(near_scores, axis=2), jnp.max(distant_scores, axis=2))[..., None]
    near_exp = jnp.exp(near_scores - row_max)
    far_exp = jnp.exp(distant_scores - row_max)
    summed = jnp.sum(near_exp, axis=2, keepdims=True) + jnp.sum(far_exp, axis=2, keepdims=True)
    near_probs = (near_exp / summed).astype(jnp.bfloat16)
    distant_probabilities = (
        (far_exp / summed)
        .astype(jnp.bfloat16)
        .reshape(head_count, BLOCKS_DEV, block_rows, list_len, block_rows)
    )
    near_term = jnp.einsum(
        "hqk,hkd->hqd", near_probs, value_own, preferred_element_type=jnp.float32
    )
    distant_partial = jnp.einsum(
        "hbqrk,hbrkd->hbqd",
        distant_probabilities,
        far_rows[..., HEAD_SIZE:],
        preferred_element_type=jnp.float32,
    )
    attended = (near_term + distant_partial.reshape(head_count, tok_rows, HEAD_SIZE)).astype(
        jnp.bfloat16
    )
    going_back = jax.vmap(
        lambda rows_in, picks: jnp.zeros((seq_count * lot_size, HEAD_SIZE), jnp.bfloat16)
        .at[picks]
        .set(rows_in)
    )(attended, held_flat)
    came_back = lax.all_to_all(
        going_back.reshape(head_count, seq_count, lot_size, HEAD_SIZE),
        "seq",
        split_axis=1,
        concat_axis=1,
        tiled=True,
    )
    came_flat = came_back.reshape(head_count, seq_count * lot_size, HEAD_SIZE)
    target = jnp.where(send_live, send_row, tok_rows).reshape(head_count, -1)
    per_head = jax.vmap(
        lambda rows_in, picks: jnp.zeros((tok_rows, HEAD_SIZE), jnp.bfloat16)
        .at[picks]
        .set(rows_in, mode="drop")
    )(came_flat, target)
    joined = per_head.transpose(1, 0, 2).reshape(tok_rows, heads_here * HEAD_SIZE)
    partial_value = jnp.dot(joined, out_weight, preferred_element_type=jnp.float32)
    return lax.psum_scatter(
        partial_value.astype(jnp.bfloat16), "head", scatter_dimension=1, tiled=True
    )


def solution(mesh):
    placed = (
        P("seq", "head"),
        P("seq", "head"),
        P("seq", "head"),
        P("head", None),
        P("head", "seq", None),
        P("head", "seq"),
        P("head", None),
    )
    return jax.shard_map(
        body, mesh=mesh, in_specs=placed, out_specs=P("seq", "head"), check_vma=False
    )
```

profile of v0, /device:TPU:0, one launch (start us, length us, event | category | flops | bytes accessed | tf_op | source)
XLA Modules:
  0.0 208.6 jit_solution(4459493861391357024)
XLA Ops:
  9.0 8.3 %all-to-all-start.1 = ((s32[16,1,3]{2,1,0:T(1,128)}), s32[16,1,3]{2,1,0:T(1,128)S(1)}, u32[]{:S(2)}, u32[]{:S(2)}) async-start(s32[16,1,3]{2,1,0:T(1,128)} %copy.99), calls=%async_computation.1 | async-start | bytes 16384 | tf_op jit(solution)/shard_map/all_to_all | solution.py:65
  17.4 0.9 reshape.244
  18.3 1.7 reduce-window.14
  22.2 0.9 fusion.1
  24.2 1.1 copy.91
  26.2 10.0 %gather_fusion.2 = bf16[1536,384]{1,0:T(8,128)(2,1)S(1)} fusion(bf16[3,256,384]{2,1,0:T(8,128)(2,1)S(1)} %maximum_bitcast_fusion, s32[1536]{0:T(1024)S(1)} %reshape.276), kind=kCustom, calls=%fused_computation.2 | custom fusion | bytes 2371584 | tf_op jit(solution)/shard_map/vmap()/gather | solution.py:42
  36.1 1.1 copy.97
  37.3 6.9 %all-to-all-start = ((bf16[3,16,32,384]{3,2,0,1:T(8,128)(2,1)}), bf16[3,16,32,384]{3,2,0,1:T(8,128)(2,1)S(1)}, u32[]{:S(2)}, u32[]{:S(2)}) async-start(bf16[3,16,32,384]{3,2,0,1:T(8,128)(2,1)} %copy.97), calls=%async_computation | async-start | bytes 2359296 | tf_op jit(solution)/shard_map/all_to_all | solution.py:47
  44.9 1.7 reduce-window.16
  48.1 22.5 %all-to-all-done = bf16[3,16,32,384]{3,2,0,1:T(8,128)(2,1)S(1)} async-done(((bf16[3,16,32,384]{3,2,0,1:T(8,128)(2,1)}), bf16[3,16,32,384]{3,2,0,1:T(8,128)(2,1)S(1)}, u32[]{:S(2)}, u32[]{:S(2)}) %all-to-all-start) | async-done | bytes 1179680 | tf_op jit(solution)/shard_map/all_to_all | solution.py:47
  70.7 5.1 %gather_fusion.3 = bf16[768,384]{1,0:T(8,128)(2,1)S(1)} fusion(bf16[3,512,384]{2,1,0:T(8,128)(2,1)S(1)} %bitcast.95, s32[768]{0:T(1024)S(1)} %reshape.282), kind=kCustom, calls=%fused_computation.3 | custom fusion | bytes 1185792 | tf_op jit(solution)/shard_map/vmap()/gather | solution.py:50
  75.8 1.9 gather_fusion
  77.7 6.3 %all-to-all-start.2 = ((bf16[16,3,64,256]{3,2,1,0:T(8,128)(2,1)}), bf16[16,3,64,256]{3,2,1,0:T(8,128)(2,1)S(1)}, u32[]{:S(2)}, u32[]{:S(2)}) async-start(bf16[16,3,64,256]{3,2,1,0:T(8,128)(2,1)} %bitcast.16), calls=%async_computation.2 | async-start | bytes 3145728 | tf_op jit(solution)/shard_map/all_to_all | solution.py:64
  84.6 32.5 %all-to-all-done.2 = bf16[16,3,64,256]{3,2,1,0:T(8,128)(2,1)S(1)} async-done(((bf16[16,3,64,256]{3,2,1,0:T(8,128)(2,1)}), bf16[16,3,64,256]{3,2,1,0:T(8,128)(2,1)S(1)}, u32[]{:S(2)}, u32[]{:S(2)}) %all-to-all-start.2) | async-done | bytes 1572896 | tf_op jit(solution)/shard_map/all_to_all | solution.py:64
  117.1 2.0 gather_fusion.1
  119.1 2.7 %fusion.43 = (f32[3,4,64]{2,1,0:T(4,128)S(1)}, f32[3,4,64,4,64]{2,4,3,1,0:T(8,128)}) fusion(bf16[3,4,64,128,1]{3,2,4,1,0:T(8,128)(2,1)S(1)} %bitcast.114, bf16[3,4,4,64,256]{4,3,2,1,0:T(8,128)(2,1)} %bitcast.103, pred[3,4,4]{2,1,0:T(4,128)(4,1)S(1)} %iota_compare_fusion.5), kind=kOutput, calls=%fused_computation.110 | convolution fusion | flops 50920704 | bytes 1772592 | tf_op jit(solution)/shard_map/hbqd,hbrkd->hbqrk/dot_general | solution.py:78
  121.9 1.8 fusion.2
  124.0 1.8 fusion.4
  126.2 37.1 %scatter_fusion = bf16[3,512,128]{2,1,0:T(8,128)(2,1)S(1)} fusion(bf16[3,512,128]{2,1,0:T(8,128)(2,1)S(1)} %broadcast_in_dim.82, s32[768]{0:T(1024)S(1)} %reshape.288, bf16[768,128]{1,0:T(8,128)(2,1)S(1)} %bitcast.113), kind=kCustom, calls=%fused_computation.4 | custom fusion | bytes 595968 | tf_op jit(solution)/shard_map/vmap()/scatter | solution.py:114
  164.1 7.4 %all-to-all-start.3 = ((bf16[3,16,32,128]{3,2,0,1:T(8,128)(2,1)}), bf16[3,16,32,128]{3,2,0,1:T(8,128)(2,1)S(1)}, u32[]{:S(2)}, u32[]{:S(2)}) async-start(bf16[3,16,32,128]{3,2,0,1:T(8,128)(2,1)} %copy.104), calls=%async_computation.3 | async-start | bytes 786432 | tf_op jit(solution)/shard_map/all_to_all | solution.py:116
  172.0 11.3 %all-to-all-done.3 = bf16[3,16,32,128]{3,2,0,1:T(8,128)(2,1)S(1)} async-done(((bf16[3,16,32,128]{3,2,0,1:T(8,128)(2,1)}), bf16[3,16,32,128]{3,2,0,1:T(8,128)(2,1)S(1)}, u32[]{:S(2)}, u32[]{:S(2)}) %all-to-all-start.3) | async-done | bytes 393248 | tf_op jit(solution)/shard_map/all_to_all | solution.py:116
  183.4 4.5 %scatter_custom_fusion.1 = bf16[768,128]{1,0:T(8,128)(2,1)S(1)} fusion(s32[1536]{0:T(1024)S(1)} %reshape.294, bf16[1536,128]{1,0:T(8,128)(2,1)S(1)} %bitcast.112, bf16[]{:T(256)} %constant.80.clone.1), kind=kCustom, calls=%fused_computation.29 | custom fusion | bytes 196610
  188.0 5.2 %convolution_convert_fusion = bf16[256,5120]{1,0:T(8,128)(2,1)} fusion(bf16[256,384]{0,1:T(8,128)(2,1)S(1)} %bitcast.105, bf16[384,5120]{1,0:T(8,128)(2,1)} %param.13), kind=kOutput, calls=%fused_computation.6 | convolution fusion | flops 1007943680 | bytes 6750208 | tf_op jit(solution)/shard_map/dot_general | solution.py:131
  193.2 8.5 %reduce-scatter.2.cloned.1.call-done = bf16[256,2560]{1,0:T(8,128)(2,1)} async-done(((bf16[256,5120]{1,0:T(8,128)(2,1)}), bf16[256,2560]{1,0:T(8,128)(2,1)}) %reduce-scatter.2.cloned.1.call-update) | async-done | bytes 1310736 | tf_op jit(solution)/shard_map/reduce_scatter | solution.py:132
  (80 shorter events, 11.6 us)
Async XLA Ops:
  6.5 18.9 %copy-start.1 = (bf16[256,384]{1,0:T(8,128)(2,1)S(1)}, bf16[256,384]{1,0:T(8,128)(2,1)}, u32[]{:S(2)}) copy-start(bf16[256,384]{1,0:T(8,128)(2,1)} %param.8) | copy-start | bytes 589828
  6.5 19.2 %copy-start.2 = (bf16[256,384]{1,0:T(8,128)(2,1)S(1)}, bf16[256,384]{1,0:T(8,128)(2,1)}, u32[]{:S(2)}) copy-start(bf16[256,384]{1,0:T(8,128)(2,1)} %param.9) | copy-start | bytes 589828
  9.0 28.3 %all-to-all-start.1 = ((s32[16,1,3]{2,1,0:T(1,128)}), s32[16,1,3]{2,1,0:T(1,128)S(1)}, u32[]{:S(2)}, u32[]{:S(2)}) async-start(s32[16,1,3]{2,1,0:T(1,128)} %copy.99), calls=%async_computation.1 | async-start | bytes 16384 | tf_op jit(solution)/shard_map/all_to_all | solution.py:65
  37.3 33.3 %all-to-all-start = ((bf16[3,16,32,384]{3,2,0,1:T(8,128)(2,1)}), bf16[3,16,32,384]{3,2,0,1:T(8,128)(2,1)S(1)}, u32[]{:S(2)}, u32[]{:S(2)}) async-start(bf16[3,16,32,384]{3,2,0,1:T(8,128)(2,1)} %copy.97), calls=%async_computation | async-start | bytes 2359296 | tf_op jit(solution)/shard_map/all_to_all | solution.py:47
  77.7 6.4 %copy-start.3 = (s32[3,4]{1,0:T(4,128)S(1)}, s32[3,4]{1,0:T(4,128)}, u32[]{:S(2)}) copy-start(s32[3,4]{1,0:T(4,128)} %param.12) | copy-start | bytes 148
  77.7 39.4 %all-to-all-start.2 = ((bf16[16,3,64,256]{3,2,1,0:T(8,128)(2,1)}), bf16[16,3,64,256]{3,2,1,0:T(8,128)(2,1)S(1)}, u32[]{:S(2)}, u32[]{:S(2)}) async-start(bf16[16,3,64,256]{3,2,1,0:T(8,128)(2,1)} %bitcast.16), calls=%async_computation.2 | async-start | bytes 3145728 | tf_op jit(solution)/shard_map/all_to_all | solution.py:64
  121.8 2.2 %copy-start = (bf16[48,64,256]{2,1,0:T(8,128)(2,1)S(1)}, bf16[48,64,256]{2,1,0:T(8,128)(2,1)}, u32[]{:S(2)}) copy-start(bf16[48,64,256]{2,1,0:T(8,128)(2,1)} %gather_fusion.1) | copy-start | bytes 4718596
  163.3 8.5 %copy-start.5 = (s32[2]{0:T(128)S(1)}, s32[2]{0:T(128)}, u32[]{:S(2)}) copy-start(s32[2]{0:T(128)} %constant.105) | copy-start | bytes 28
  163.4 8.6 %copy-start.4 = (s32[2]{0:T(128)S(1)}, s32[2]{0:T(128)}, u32[]{:S(2)}) copy-start(s32[2]{0:T(128)} %constant.108) | copy-start | bytes 28
  164.1 19.2 %all-to-all-start.3 = ((bf16[3,16,32,128]{3,2,0,1:T(8,128)(2,1)}), bf16[3,16,32,128]{3,2,0,1:T(8,128)(2,1)S(1)}, u32[]{:S(2)}, u32[]{:S(2)}) async-start(bf16[3,16,32,128]{3,2,0,1:T(8,128)(2,1)} %copy.104), calls=%async_computation.3 | async-start | bytes 786432 | tf_op jit(solution)/shard_map/all_to_all | solution.py:116
  171.6 30.1 %reduce-scatter.2.cloned.1.call-start = ((), (), s32[]{:S(2)}) async-start(), calls=%async_computation.5 | async-start | bytes 3932160 | tf_op jit(solution)/shard_map/reduce_scatter | solution.py:132
Sparse Core Ops, SparseCore 0:
  193.4 8.3 reduce-scatter.1
where the time goes:
time: 209 us
  waiting for transfers between devices  74.9 us (36%)
  local copies, waits for them, and re-layouts  67.9 us (32%)
  starting transfers between devices  29.2 us (14%)
  between operations  13.7 us (7%)
  other arithmetic  12.6 us (6%)
  matrix products  10.3 us (5%)
    scatter x3, local copies, waits for them, and re-layouts, body(): going_back = jax.vmap(lambda rows_in, picks: jnp.zeros((seq_count * lot_s...  37.1 us
    all_to_all x1, waiting for transfers between devices, body(): lax.all_to_all(blocks_flat[lax.all_to_all(wanted.T, 'seq', split_axis=0,...  32.5 us
    all_to_all x1, waiting for transfers between devices, body(): lax.all_to_all(outgoing, 'seq', split_axis=1, concat_axis=1, tiled=True)  22.5 us
    gather x3, local copies, waits for them, and re-layouts, body(): table[picks]  15.1 us
    all_to_all x1, waiting for transfers between devices, body(): lax.all_to_all(going_back.reshape(head_count, seq_count, lot_size, HEAD_S...  11.3 us
    reduce_scatter x1, waiting for transfers between devices, body(): lax.psum_scatter(partial_value.astype(jnp.bfloat16), 'head', scatter_dime...  8.48 us
    all_to_all x1, starting transfers between devices, body(): lax.all_to_all(wanted.T, 'seq', split_axis=0, concat_axis=0, tiled=True)  8.34 us
    all_to_all x1, starting transfers between devices, body(): lax.all_to_all(going_back.reshape(head_count, seq_count, lot_size, HEAD_S...  7.43 us
  transfers between devices with their start and end apart: 5, of which 4 were waited for; matrix products, arithmetic and copies ran while one was open for 12% of the time, Pallas kernels for 0%

commit v1 on v0

--- a/solution.py
+++ b/solution.py
@@ -1,15 +1,18 @@
+import functools
 import math
 
 import jax
 import jax.numpy as jnp
 from jax import lax
+from jax.experimental import pallas as pl
+from jax.experimental.pallas import tpu as pltpu
 from jax.sharding import PartitionSpec as P
 
 HEAD_SIZE = 128
 BLOCKS_DEV = 4
 
 
-def body(queries, keys, values, token_perm, pair_blocks, pair_counts, out_weight):
+def plain_body(queries, keys, values, token_perm, pair_blocks, pair_counts, out_weight):
     tok_rows = queries.shape[0]
     heads_here = token_perm.shape[0]
     list_len = pair_blocks.shape[2]
@@ -134,6 +137,319 @@
     )
 
 
+MESH = pl.DeviceIdType.MESH
+NN = (((1,), (0,)), ((), ()))
+NT = (((1,), (1,)), ((), ()))
+ROW_PAD = 8
+
+
+def matmul(a, b, dims=NN):
+    return lax.dot_general(a, b, dims, preferred_element_type=jnp.float32)
+
+
+def one_hot(mask):
+    return jnp.where(mask, 1.0, 0.0).astype(jnp.bfloat16)
+
+
+def iota(shape, axis):
+    return lax.broadcasted_iota(jnp.int32, shape, axis)
+
+
+def kernel(
+    seq_count, heads, lot, list_len,
+    q_ref, k_ref, v_ref, perm_ref, pairs_ref, counts_ref, w_ref, out_ref,
+    perm_rows, code_rows, local_rows, pick, pick_t, place, place_t,
+    want_out, want_in, want_s, kv_out, kv_in, q_out, q_in, own_kv,
+    far_out, far_in, near_o, near_m, near_l, own_q, attended, back_out, back_in,
+    joined_own, joined_other, w_own, w_other,
+    sends, recvs, w_sems, j_send, j_recv, want_sem,
+):
+    tok = q_ref.shape[0]
+    size = HEAD_SIZE
+    block = tok // BLOCKS_DEV
+    slots = seq_count * lot
+    cols = out_ref.shape[1]
+    me = lax.axis_index("seq")
+    side = lax.axis_index("head")
+    scale = 1.0 / math.sqrt(HEAD_SIZE)
+    kv_phase, q_phase, want_phase, far_phase = 0, 1, 2, 3
+    back_phase = far_phase + heads
+
+    barrier = pltpu.get_barrier_semaphore()
+
+    @pl.loop(1, seq_count)
+    def _(k):
+        pl.semaphore_signal(
+            barrier, inc=1, device_id={"seq": lax.rem(me + k, seq_count)}, device_id_type=MESH
+        )
+
+    pl.semaphore_signal(barrier, inc=1, device_id={"head": 1 - side}, device_id_type=MESH)
+
+    own_cols = pl.ds(pl.multiple_of(side * cols, 128), cols)
+    other_cols = pl.ds(pl.multiple_of((1 - side) * cols, 128), cols)
+    w_local = pltpu.make_async_copy(w_ref.at[:, own_cols], w_own, w_sems.at[0])
+    w_local.start()
+
+    def push(phase, k, source, target):
+        dst = lax.rem(me + k, seq_count)
+        return pltpu.make_async_remote_copy(
+            src_ref=source.at[dst],
+            dst_ref=target.at[me],
+            send_sem=sends.at[phase, k],
+            recv_sem=recvs.at[phase, k],
+            device_id={"seq": dst},
+            device_id_type=MESH,
+        )
+
+    def start_all(phase, source, target):
+        @pl.loop(1, seq_count)
+        def _(k):
+            push(phase, k, source, target).start()
+
+    def wait_all(phase, source, target):
+        @pl.loop(1, seq_count)
+        def _(k):
+            push(phase, k, source, target).wait_recv()
+
+    def sent_all(phase, source, target):
+        @pl.loop(1, seq_count)
+        def _(k):
+            push(phase, k, source, target).wait_send()
+
+    owner_ids = iota((seq_count, 1, 128), 0)
+    head_lanes = iota((seq_count, 1, 128), 2)
+    want = jnp.zeros((seq_count, 1, 128), jnp.int32)
+    for h in range(heads):
+        for b in range(BLOCKS_DEV):
+            for r in range(list_len):
+                entry = pairs_ref[h, b, r]
+                owner = lax.div(entry, BLOCKS_DEV)
+                code = entry - owner * BLOCKS_DEV + BLOCKS_DEV * h
+                want = jnp.where((owner_ids == owner) & (head_lanes == h), code, want)
+    want_out[...] = want
+
+    perm_rows[...] = jnp.zeros_like(perm_rows)
+    for o in range(seq_count):
+        perm_rows[o * ROW_PAD : o * ROW_PAD + heads, :] = perm_ref[:, o * tok : (o + 1) * tok]
+    before = one_hot(iota((tok, tok), 0) < iota((tok, tok), 1))
+    local = perm_rows[...] - me * tok
+    from_here = (local >= 0) & (local < tok)
+    rank = matmul(one_hot(from_here), before)
+    code_rows[...] = jnp.where(from_here, rank, -1.0)
+    local_rows[...] = local.astype(jnp.float32)
+    slot_ids = iota((lot, tok), 0).astype(jnp.float32)
+    lane_ids = iota((lot, tok), 1).astype(jnp.float32)
+    for o in range(seq_count):
+        for h in range(heads):
+            row = o * ROW_PAD + h
+            hit = slot_ids == code_rows[row : row + 1, :]
+            picked = (
+                jnp.sum(
+                    jnp.where(hit, local_rows[row : row + 1, :] + 1.0, 0.0), axis=1, keepdims=True
+                )
+                - 1.0
+            )
+            pick[h, o * lot : (o + 1) * lot, :] = one_hot(lane_ids == picked)
+
+    for h in range(heads):
+        hc = slice(h * size, (h + 1) * size)
+        for half, ref in ((0, k_ref), (1, v_ref)):
+            rows = matmul(pick[h], ref[:, hc]).astype(jnp.bfloat16)
+            kv_out[:, h * lot : (h + 1) * lot, half * size : (half + 1) * size] = rows.reshape(
+                seq_count, lot, size
+            )
+
+    pl.semaphore_wait(barrier, seq_count)
+    start_all(want_phase, want_out, want_in)
+    start_all(kv_phase, kv_out, kv_in)
+    for h in range(heads):
+        rows = matmul(pick[h], q_ref[:, h * size : (h + 1) * size]).astype(jnp.bfloat16)
+        q_out[:, h * lot : (h + 1) * lot, :] = rows.reshape(seq_count, lot, size)
+    start_all(q_phase, q_out, q_in)
+    w_remote = pltpu.make_async_remote_copy(
+        src_ref=w_ref.at[:, other_cols],
+        dst_ref=w_other,
+        send_sem=w_sems.at[1],
+        recv_sem=w_sems.at[2],
+        device_id={"head": 1 - side},
+        device_id_type=MESH,
+    )
+    w_remote.start()
+
+    mine = perm_rows[pl.ds(pl.multiple_of(me * ROW_PAD, ROW_PAD), ROW_PAD), :]
+    source_ids = iota((seq_count, tok), 0)
+    flats = []
+    for h in range(heads):
+        gap = mine[h : h + 1, :] - source_ids * tok
+        hot = (gap >= 0) & (gap < tok)
+        place_of = matmul(one_hot(hot), before) + (source_ids * lot).astype(jnp.float32)
+        flat = jnp.sum(jnp.where(hot, place_of, 0.0), axis=0, keepdims=True)
+        place_t[h] = one_hot(iota((slots, tok), 0).astype(jnp.float32) == flat)
+        flats.append(flat)
+    flats = jnp.concatenate(
+        [jnp.broadcast_to(f, (ROW_PAD, tok)) for f in flats], axis=0
+    ).T
+    for h in range(heads):
+        column = flats[:, h * ROW_PAD : h * ROW_PAD + 1]
+        place[h] = one_hot(iota((tok, slots), 1).astype(jnp.float32) == column)
+        pick_t[h] = pick[h].T
+    kv_in[me] = kv_out[me]
+    q_in[me] = q_out[me]
+
+    wait_all(want_phase, want_out, want_in)
+    want_in[me] = want_out[me]
+    to_scalars = pltpu.make_async_copy(want_in, want_s, want_sem)
+    to_scalars.start()
+    to_scalars.wait()
+
+    wait_all(kv_phase, kv_out, kv_in)
+    for h in range(heads):
+        lots = kv_in[:, h * lot : (h + 1) * lot, :].reshape(slots, 2 * size)
+        rows = matmul(place[h], lots).astype(jnp.bfloat16)
+        own_kv[h * BLOCKS_DEV : (h + 1) * BLOCKS_DEV] = rows.reshape(BLOCKS_DEV, block, 2 * size)
+
+        @pl.loop(1, seq_count)
+        def _(k):
+            dst = lax.rem(me + k, seq_count)
+            far_out[h, dst] = own_kv[want_s[dst, 0, h]]
+
+        start_all(far_phase + h, far_out.at[h], far_in[h])
+
+    wait_all(q_phase, q_out, q_in)
+    for h in range(heads):
+        lots = q_in[:, h * lot : (h + 1) * lot, :].reshape(slots, size)
+        query = matmul(place[h], lots).astype(jnp.bfloat16)
+        own_q[h] = query
+        kv = own_kv[h * BLOCKS_DEV : (h + 1) * BLOCKS_DEV].reshape(tok, 2 * size)
+        scores = matmul(query, kv[:, :size], NT) * scale
+        top = jnp.max(scores, axis=1, keepdims=True)
+        weights = jnp.exp(scores - top)
+        near_m[h] = top
+        near_l[h] = jnp.sum(weights, axis=1, keepdims=True)
+        near_o[h] = matmul(weights.astype(jnp.bfloat16), kv[:, size:])
+
+    far_lanes = iota((block, list_len * block), 1)
+    for h in range(heads):
+        wait_all(far_phase + h, far_out.at[h], far_in[h])
+        for b in range(BLOCKS_DEV):
+            rows = slice(b * block, (b + 1) * block)
+            far = jnp.concatenate(
+                [far_in[h][lax.div(pairs_ref[h, b, r], BLOCKS_DEV)] for r in range(list_len)], axis=0
+            )
+            scores = matmul(own_q[h, rows, :], far[:, :size], NT) * scale
+            scores = jnp.where(far_lanes < counts_ref[h, b] * block, scores, -1e30)
+            near_top = near_m[h, rows, :]
+            top = jnp.maximum(near_top, jnp.max(scores, axis=1, keepdims=True))
+            weights = jnp.exp(scores - top)
+            shrink = jnp.exp(near_top - top)
+            total = near_l[h, rows, :] * shrink + jnp.sum(weights, axis=1, keepdims=True)
+            mixed = near_o[h, rows, :] * shrink + matmul(
+                weights.astype(jnp.bfloat16), far[:, size:]
+            )
+            attended[rows, :] = (mixed / total).astype(jnp.bfloat16)
+        back = matmul(place_t[h], attended[...]).astype(jnp.bfloat16)
+        back_out[h] = back.reshape(seq_count, lot, size)
+        start_all(back_phase + h, back_out.at[h], back_in.at[h])
+        back_in[h, me] = back_out[h, me]
+
+    to_other = []
+    for h in range(heads):
+        wait_all(back_phase + h, back_out.at[h], back_in.at[h])
+        joined_own[h] = matmul(pick_t[h], back_in[h].reshape(slots, size)).astype(jnp.bfloat16)
+        copy = pltpu.make_async_remote_copy(
+            src_ref=joined_own.at[h],
+            dst_ref=joined_other.at[h],
+            send_sem=j_send.at[h],
+            recv_sem=j_recv.at[h],
+            device_id={"head": 1 - side},
+            device_id_type=MESH,
+        )
+        copy.start()
+        to_other.append(copy)
+    w_local.wait()
+    w_remote.wait_recv()
+    step = 512 if cols % 512 == 0 else 128
+    for copy in to_other:
+        copy.wait_recv()
+    left = jnp.concatenate([joined_own[h] for h in range(heads)], axis=1)
+    right = jnp.concatenate([joined_other[h] for h in range(heads)], axis=1)
+    for c in range(0, cols, step):
+        own_part = matmul(left, w_own[:, c : c + step]).astype(jnp.bfloat16)
+        other_part = matmul(right, w_other[:, c : c + step]).astype(jnp.bfloat16)
+        out_ref[:, c : c + step] = (
+            own_part.astype(jnp.float32) + other_part.astype(jnp.float32)
+        ).astype(jnp.bfloat16)
+
+    for copy in to_other:
+        copy.wait_send()
+    w_remote.wait_send()
+    sent_all(want_phase, want_out, want_in)
+    sent_all(kv_phase, kv_out, kv_in)
+    sent_all(q_phase, q_out, q_in)
+    for h in range(heads):
+        sent_all(far_phase + h, far_out.at[h], far_in[h])
+        sent_all(back_phase + h, back_out.at[h], back_in.at[h])
+
+
+def body(queries, keys, values, token_perm, pair_blocks, pair_counts, out_weight):
+    tok = queries.shape[0]
+    heads = token_perm.shape[0]
+    list_len = pair_blocks.shape[2]
+    seq_count = lax.axis_size("seq")
+    lot = 2 * tok // seq_count
+    block = tok // BLOCKS_DEV
+    slots = seq_count * lot
+    size = HEAD_SIZE
+    width = out_weight.shape[1]
+    cols = width // 2
+    vmem = pl.BlockSpec(memory_space=pltpu.VMEM)
+    smem = pl.BlockSpec(memory_space=pltpu.SMEM)
+    bf16, f32, i32 = jnp.bfloat16, jnp.float32, jnp.int32
+    return pl.pallas_call(
+        functools.partial(kernel, seq_count, heads, lot, list_len),
+        out_shape=jax.ShapeDtypeStruct((tok, cols), bf16),
+        in_specs=[vmem] * 4 + [smem] * 2 + [pl.BlockSpec(memory_space=pl.ANY)],
+        out_specs=vmem,
+        scratch_shapes=[
+            pltpu.VMEM((seq_count * ROW_PAD, tok), i32),
+            pltpu.VMEM((seq_count * ROW_PAD, tok), f32),
+            pltpu.VMEM((seq_count * ROW_PAD, tok), f32),
+            pltpu.VMEM((heads, slots, tok), bf16),
+            pltpu.VMEM((heads, tok, slots), bf16),
+            pltpu.VMEM((heads, tok, slots), bf16),
+            pltpu.VMEM((heads, slots, tok), bf16),
+            pltpu.VMEM((seq_count, 1, 128), i32),
+            pltpu.VMEM((seq_count, 1, 128), i32),
+            pltpu.SMEM((seq_count, 1, 128), i32),
+            pltpu.VMEM((seq_count, heads * lot, 2 * size), bf16),
+            pltpu.VMEM((seq_count, heads * lot, 2 * size), bf16),
+            pltpu.VMEM((seq_count, heads * lot, size), bf16),
+            pltpu.VMEM((seq_count, heads * lot, size), bf16),
+            pltpu.VMEM((heads * BLOCKS_DEV, block, 2 * size), bf16),
+            pltpu.VMEM((heads, seq_count, block, 2 * size), bf16),
+            [pltpu.VMEM((seq_count, block, 2 * size), bf16)] * heads,
+            pltpu.VMEM((heads, tok, size), f32),
+            pltpu.VMEM((heads, tok, 1), f32),
+            pltpu.VMEM((heads, tok, 1), f32),
+            pltpu.VMEM((heads, tok, size), bf16),
+            pltpu.VMEM((tok, size), bf16),
+            pltpu.VMEM((heads, seq_count, lot, size), bf16),
+            pltpu.VMEM((heads, seq_count, lot, size), bf16),
+            pltpu.VMEM((heads, tok, size), bf16),
+            pltpu.VMEM((heads, tok, size), bf16),
+            pltpu.VMEM((heads * size, cols), bf16),
+            pltpu.VMEM((heads * size, cols), bf16),
+            pltpu.SemaphoreType.DMA((3 + 2 * heads, seq_count)),
+            pltpu.SemaphoreType.DMA((3 + 2 * heads, seq_count)),
+            pltpu.SemaphoreType.DMA((3,)),
+            pltpu.SemaphoreType.DMA((heads,)),
+            pltpu.SemaphoreType.DMA((heads,)),
+            pltpu.SemaphoreType.DMA,
+        ],
+        compiler_params=pltpu.CompilerParams(collective_id=0, has_side_effects=True),
+    )(queries, keys, values, token_perm, pair_blocks, pair_counts, out_weight)
+
+
 def solution(mesh):
     placed = (
         P("seq", "head"),
@@ -144,6 +460,13 @@
         P("head", "seq"),
         P("head", None),
     )
-    return jax.shard_map(
-        body, mesh=mesh, in_specs=placed, out_specs=P("seq", "head"), check_vma=False
-    )
+
+    def run(queries, keys, values, token_perm, pair_blocks, pair_counts, out_weight):
+        seq_count, head_groups = mesh.shape["seq"], mesh.shape["head"]
+        lot = 2 * (queries.shape[0] // seq_count) // seq_count
+        one = body if lot % 16 == 0 and head_groups == 2 else plain_body
+        return jax.shard_map(
+            one, mesh=mesh, in_specs=placed, out_specs=P("seq", "head"), check_vma=False
+        )(queries, keys, values, token_perm, pair_blocks, pair_counts, out_weight)
+
+    return run

time: 209 us -> 90.8 us (0.43)
  Pallas kernels: 0 us -> 87.4 us
  waiting for transfers between devices: 74.9 us -> 0 us
  local copies, waits for them, and re-layouts: 67.9 us -> 2.46 us
  starting transfers between devices: 29.2 us -> 0 us
  between operations: 13.7 us -> 0.01 us
  other arithmetic: 12.6 us -> 0 us
  matrix products: 10.3 us -> 0 us
    pallas_call x0 -> x1, Pallas kernels: none -> 87.4 us  [body(): pl.pallas_call(functools.partial(kernel, seq_count, heads, lot, list_len)...]
    all_to_all x4 -> x0, waiting for transfers between devices: 66.4 us -> none  [the longest x1 32.5 us: body(): lax.all_to_all(blocks_flat[lax.all_to_all(wanted.T, 'seq', split_axis=0,...]
    scatter x3 -> x0, local copies, waits for them, and re-layouts: 37.1 us -> none  [body(): going_back = jax.vmap(lambda rows_in, picks: jnp.zeros((seq_count * lot_s...]
    all_to_all x4 -> x0, starting transfers between devices: 29 us -> none  [the longest x1 8.34 us: body(): lax.all_to_all(wanted.T, 'seq', split_axis=0, concat_axis=0, tiled=True)]
    gather x5 -> x0, local copies, waits for them, and re-layouts: 18.9 us -> none  [the longest x3 15.1 us: body(): table[picks]]
    dot_general x5 -> x0, matrix products: 10.3 us -> none  [the longest x1 5.17 us: body(): jnp.dot(joined, out_weight, preferred_element_type=jnp.float32)]
    reduce_scatter x1 -> x0, waiting for transfers between devices: 8.48 us -> none  [body(): lax.psum_scatter(partial_value.astype(jnp.bfloat16), 'head', scatter_dime...]
    another operation x4 -> x0, other arithmetic: 3.52 us -> none
  transfers between devices with their start and end apart: 5 -> 0, of which waited for: 4 -> 0; matrix products, arithmetic and copies ran while one was open for 12% -> 0% of each run, Pallas kernels for 0% -> 0%
where the time goes in v1:
time: 90.8 us; the launch traced here: 89.8 us
  Pallas kernels  87.4 us (96%)
  local copies, waits for them, and re-layouts  2.46 us (3%)
    pallas_call x1, Pallas kernels, body(): pl.pallas_call(functools.partial(kernel, seq_count, heads, lot, list_len)...  87.4 us
    unnamed x1, local copies, waits for them, and re-layouts  2.46 us

profile of v1, /device:TPU:0, one launch (start us, length us, event | category | flops | bytes accessed | tf_op | source)
XLA Modules:
  0.0 89.8 jit_solution(12956997935878518480)
XLA Ops:
  0.0 87.4 %shard_map.73 = bf16[256,2560]{1,0:T(8,128)(2,1)} custom-call(bf16[256,384]{1,0:T(8,128)(2,1)} %q_ref.1, bf16[256,384]{1,0:T(8,128)(2,1)} %k_ref.1, bf16[256,384]{1,0:T(8,128)(2,1)} %v_ref.1, s32[3,4096]{1,0:T(4,128)} %perm_ref.1, s32[3,4,4]{2,1,0:T(4,128)} %pairs_ref.1, s32[3,4]{1,0:T(4,128)} %counts_ref.1, bf16[384,5120]{1,0:T(8,128)(2,1)} %w_ref.1), custom_call_target="tpu_custom_call" | custom-call | tf_op jit(solution)/shard_map/pallas_call | solution.py:408
  87.4 2.5 %copy.9 = bf16[256,2560]{1,0:T(8,128)(2,1)} copy(bf16[256,2560]{1,0:T(8,128)(2,1)} %shard_map.73) | data formatting | bytes 2621440

commit v2 on v1

--- a/solution.py
+++ b/solution.py
@@ -162,7 +162,7 @@
     want_out, want_in, want_s, kv_out, kv_in, q_out, q_in, own_kv,
     far_out, far_in, near_o, near_m, near_l, own_q, attended, back_out, back_in,
     joined_own, joined_other, w_own, w_other,
-    sends, recvs, w_sems, j_send, j_recv, want_sem,
+    mirror_kv, sends, recvs, w_sems, j_send, j_recv, m_send, m_recv, want_sem,
 ):
     tok = q_ref.shape[0]
     size = HEAD_SIZE
@@ -173,7 +173,11 @@
     side = lax.axis_index("head")
     scale = 1.0 / math.sqrt(HEAD_SIZE)
     kv_phase, q_phase, want_phase, far_phase = 0, 1, 2, 3
-    back_phase = far_phase + heads
+    relay_phase = far_phase + heads
+    back_phase = relay_phase + heads
+    half = seq_count // 2
+    base = (me // half) * half
+    mirror = lax.rem(me + half, seq_count)
 
     barrier = pltpu.get_barrier_semaphore()
 
@@ -216,7 +220,44 @@
         def _(k):
             push(phase, k, source, target).wait_send()
 
+    def push_near(phase, k, source, target, shift=0):
+        dst = base + lax.rem(me - base + k, half)
+        return pltpu.make_async_remote_copy(
+            src_ref=source.at[lax.rem(dst + shift, seq_count)],
+            dst_ref=target.at[lax.rem(me + shift, seq_count)],
+            send_sem=sends.at[phase, k],
+            recv_sem=recvs.at[phase, k],
+            device_id={"seq": dst},
+            device_id_type=MESH,
+        )
+
+    def start_near(*args):
+        @pl.loop(1, half)
+        def _(k):
+            push_near(args[0], k, *args[1:]).start()
+
+    def wait_near(*args):
+        @pl.loop(1, half)
+        def _(k):
+            push_near(args[0], k, *args[1:]).wait_recv()
+
+    def sent_near(*args):
+        @pl.loop(1, half)
+        def _(k):
+            push_near(args[0], k, *args[1:]).wait_send()
+
+    def to_mirror(h):
+        return pltpu.make_async_remote_copy(
+            src_ref=own_kv[h],
+            dst_ref=mirror_kv[h],
+            send_sem=m_send.at[h],
+            recv_sem=m_recv.at[h],
+            device_id={"seq": mirror},
+            device_id_type=MESH,
+        )
+
     owner_ids = iota((seq_count, 1, 128), 0)
+    mirror_ids = jnp.where(owner_ids < half, owner_ids + half, owner_ids - half)
     head_lanes = iota((seq_count, 1, 128), 2)
     want = jnp.zeros((seq_count, 1, 128), jnp.int32)
     for h in range(heads):
@@ -224,8 +265,9 @@
             for r in range(list_len):
                 entry = pairs_ref[h, b, r]
                 owner = lax.div(entry, BLOCKS_DEV)
-                code = entry - owner * BLOCKS_DEV + BLOCKS_DEV * h
+                code = entry - owner * BLOCKS_DEV
                 want = jnp.where((owner_ids == owner) & (head_lanes == h), code, want)
+                want = jnp.where((mirror_ids == owner) & (head_lanes == heads + h), code, want)
     want_out[...] = want
 
     perm_rows[...] = jnp.zeros_like(perm_rows)
@@ -253,14 +295,14 @@
 
     for h in range(heads):
         hc = slice(h * size, (h + 1) * size)
-        for half, ref in ((0, k_ref), (1, v_ref)):
+        for part, ref in ((0, k_ref), (1, v_ref)):
             rows = matmul(pick[h], ref[:, hc]).astype(jnp.bfloat16)
-            kv_out[:, h * lot : (h + 1) * lot, half * size : (half + 1) * size] = rows.reshape(
+            kv_out[:, h * lot : (h + 1) * lot, part * size : (part + 1) * size] = rows.reshape(
                 seq_count, lot, size
             )
 
     pl.semaphore_wait(barrier, seq_count)
-    start_all(want_phase, want_out, want_in)
+    start_near(want_phase, want_out, want_in)
     start_all(kv_phase, kv_out, kv_in)
     for h in range(heads):
         rows = matmul(pick[h], q_ref[:, h * size : (h + 1) * size]).astype(jnp.bfloat16)
@@ -296,7 +338,7 @@
     kv_in[me] = kv_out[me]
     q_in[me] = q_out[me]
 
-    wait_all(want_phase, want_out, want_in)
+    wait_near(want_phase, want_out, want_in)
     want_in[me] = want_out[me]
     to_scalars = pltpu.make_async_copy(want_in, want_s, want_sem)
     to_scalars.start()
@@ -306,21 +348,23 @@
     for h in range(heads):
         lots = kv_in[:, h * lot : (h + 1) * lot, :].reshape(slots, 2 * size)
         rows = matmul(place[h], lots).astype(jnp.bfloat16)
-        own_kv[h * BLOCKS_DEV : (h + 1) * BLOCKS_DEV] = rows.reshape(BLOCKS_DEV, block, 2 * size)
-
-        @pl.loop(1, seq_count)
-        def _(k):
-            dst = lax.rem(me + k, seq_count)
-            far_out[h, dst] = own_kv[want_s[dst, 0, h]]
-
-        start_all(far_phase + h, far_out.at[h], far_in[h])
+        own_kv[h][...] = rows.reshape(BLOCKS_DEV, block, 2 * size)
+
+        to_mirror(h).start()
+
+        @pl.loop(1, half)
+        def _(k):
+            dst = base + lax.rem(me - base + k, half)
+            far_out[h, dst] = own_kv[h][want_s[dst, 0, h]]
+
+        start_near(far_phase + h, far_out.at[h], far_in[h])
 
     wait_all(q_phase, q_out, q_in)
     for h in range(heads):
         lots = q_in[:, h * lot : (h + 1) * lot, :].reshape(slots, size)
         query = matmul(place[h], lots).astype(jnp.bfloat16)
         own_q[h] = query
-        kv = own_kv[h * BLOCKS_DEV : (h + 1) * BLOCKS_DEV].reshape(tok, 2 * size)
+        kv = own_kv[h][...].reshape(tok, 2 * size)
         scores = matmul(query, kv[:, :size], NT) * scale
         top = jnp.max(scores, axis=1, keepdims=True)
         weights = jnp.exp(scores - top)
@@ -329,8 +373,21 @@
         near_o[h] = matmul(weights.astype(jnp.bfloat16), kv[:, size:])
 
     far_lanes = iota((block, list_len * block), 1)
-    for h in range(heads):
-        wait_all(far_phase + h, far_out.at[h], far_in[h])
+
+    def relay(h):
+        to_mirror(h).wait_recv()
+
+        @pl.loop(1, half)
+        def _(k):
+            dst = base + lax.rem(me - base + k, half)
+            far_out[h, lax.rem(dst + half, seq_count)] = mirror_kv[h][want_s[dst, 0, heads + h]]
+
+        start_near(relay_phase + h, far_out.at[h], far_in[h], half)
+        far_in[h][mirror] = mirror_kv[h][want_s[me, 0, heads + h]]
+
+    def attend(h):
+        wait_near(far_phase + h, far_out.at[h], far_in[h])
+        wait_near(relay_phase + h, far_out.at[h], far_in[h], half)
         for b in range(BLOCKS_DEV):
             rows = slice(b * block, (b + 1) * block)
             far = jnp.concatenate(
@@ -351,6 +408,12 @@
         back_out[h] = back.reshape(seq_count, lot, size)
         start_all(back_phase + h, back_out.at[h], back_in.at[h])
         back_in[h, me] = back_out[h, me]
+
+    for h in range(heads):
+        relay(h)
+        if h > 0:
+            attend(h - 1)
+    attend(heads - 1)
 
     to_other = []
     for h in range(heads):
@@ -383,11 +446,13 @@
     for copy in to_other:
         copy.wait_send()
     w_remote.wait_send()
-    sent_all(want_phase, want_out, want_in)
+    sent_near(want_phase, want_out, want_in)
     sent_all(kv_phase, kv_out, kv_in)
     sent_all(q_phase, q_out, q_in)
     for h in range(heads):
-        sent_all(far_phase + h, far_out.at[h], far_in[h])
+        to_mirror(h).wait_send()
+        sent_near(far_phase + h, far_out.at[h], far_in[h])
+        sent_near(relay_phase + h, far_out.at[h], far_in[h], half)
         sent_all(back_phase + h, back_out.at[h], back_in.at[h])
 
 
@@ -425,7 +490,7 @@
             pltpu.VMEM((seq_count, heads * lot, 2 * size), bf16),
             pltpu.VMEM((seq_count, heads * lot, size), bf16),
             pltpu.VMEM((seq_count, heads * lot, size), bf16),
-            pltpu.VMEM((heads * BLOCKS_DEV, block, 2 * size), bf16),
+            [pltpu.VMEM((BLOCKS_DEV, block, 2 * size), bf16)] * heads,
             pltpu.VMEM((heads, seq_count, block, 2 * size), bf16),
             [pltpu.VMEM((seq_count, block, 2 * size), bf16)] * heads,
             pltpu.VMEM((heads, tok, size), f32),
@@ -439,9 +504,12 @@
             pltpu.VMEM((heads, tok, size), bf16),
             pltpu.VMEM((heads * size, cols), bf16),
             pltpu.VMEM((heads * size, cols), bf16),
-            pltpu.SemaphoreType.DMA((3 + 2 * heads, seq_count)),
-            pltpu.SemaphoreType.DMA((3 + 2 * heads, seq_count)),
+            [pltpu.VMEM((BLOCKS_DEV, block, 2 * size), bf16)] * heads,
+            pltpu.SemaphoreType.DMA((3 + 3 * heads, seq_count)),
+            pltpu.SemaphoreType.DMA((3 + 3 * heads, seq_count)),
             pltpu.SemaphoreType.DMA((3,)),
+            pltpu.SemaphoreType.DMA((heads,)),
+            pltpu.SemaphoreType.DMA((heads,)),
             pltpu.SemaphoreType.DMA((heads,)),
             pltpu.SemaphoreType.DMA((heads,)),
             pltpu.SemaphoreType.DMA,

time: 90.8 us -> 81.7 us (0.90)
  Pallas kernels: 87.4 us -> 78.3 us
    pallas_call x1, Pallas kernels: 87.4 us -> 78.3 us  [body(): pl.pallas_call(functools.partial(kernel, seq_count, heads, lot, list_len)...]
where the time goes in v2:
time: 81.7 us; the launch traced here: 80.8 us
  Pallas kernels  78.3 us (96%)
  local copies, waits for them, and re-layouts  2.46 us (3%)
    pallas_call x1, Pallas kernels, body(): pl.pallas_call(functools.partial(kernel, seq_count, heads, lot, list_len)...  78.3 us
    unnamed x1, local copies, waits for them, and re-layouts  2.46 us

profile of v2, /device:TPU:0, one launch (start us, length us, event | category | flops | bytes accessed | tf_op | source)
XLA Modules:
  0.0 80.8 jit_solution(7775447997625568909)
XLA Ops:
  0.0 78.3 %shard_map.73 = bf16[256,2560]{1,0:T(8,128)(2,1)} custom-call(bf16[256,384]{1,0:T(8,128)(2,1)} %q_ref.1, bf16[256,384]{1,0:T(8,128)(2,1)} %k_ref.1, bf16[256,384]{1,0:T(8,128)(2,1)} %v_ref.1, s32[3,4096]{1,0:T(4,128)} %perm_ref.1, s32[3,4,4]{2,1,0:T(4,128)} %pairs_ref.1, s32[3,4]{1,0:T(4,128)} %counts_ref.1, bf16[384,5120]{1,0:T(8,128)(2,1)} %w_ref.1), custom_call_target="tpu_custom_call" | custom-call | tf_op jit(solution)/shard_map/pallas_call | solution.py:473
  78.3 2.5 %copy.9 = bf16[256,2560]{1,0:T(8,128)(2,1)} copy(bf16[256,2560]{1,0:T(8,128)(2,1)} %shard_map.73) | data formatting | bytes 2621440

commit v3 on v2

--- a/solution.py
+++ b/solution.py
@@ -318,6 +318,10 @@
     )
     w_remote.start()
 
+    kv_in[me] = kv_out[me]
+    q_in[me] = q_out[me]
+    want_in[me] = want_out[me]
+
     mine = perm_rows[pl.ds(pl.multiple_of(me * ROW_PAD, ROW_PAD), ROW_PAD), :]
     source_ids = iota((seq_count, tok), 0)
     flats = []
@@ -335,11 +339,8 @@
         column = flats[:, h * ROW_PAD : h * ROW_PAD + 1]
         place[h] = one_hot(iota((tok, slots), 1).astype(jnp.float32) == column)
         pick_t[h] = pick[h].T
-    kv_in[me] = kv_out[me]
-    q_in[me] = q_out[me]
 
     wait_near(want_phase, want_out, want_in)
-    want_in[me] = want_out[me]
     to_scalars = pltpu.make_async_copy(want_in, want_s, want_sem)
     to_scalars.start()
     to_scalars.wait()
@@ -430,18 +431,18 @@
         copy.start()
         to_other.append(copy)
     w_local.wait()
+    step = 512 if cols % 512 == 0 else 128
+    left = jnp.concatenate([joined_own[h] for h in range(heads)], axis=1)
+    for c in range(0, cols, step):
+        out_ref[:, c : c + step] = matmul(left, w_own[:, c : c + step]).astype(jnp.bfloat16)
     w_remote.wait_recv()
-    step = 512 if cols % 512 == 0 else 128
     for copy in to_other:
         copy.wait_recv()
-    left = jnp.concatenate([joined_own[h] for h in range(heads)], axis=1)
     right = jnp.concatenate([joined_other[h] for h in range(heads)], axis=1)
     for c in range(0, cols, step):
-        own_part = matmul(left, w_own[:, c : c + step]).astype(jnp.bfloat16)
         other_part = matmul(right, w_other[:, c : c + step]).astype(jnp.bfloat16)
-        out_ref[:, c : c + step] = (
-            own_part.astype(jnp.float32) + other_part.astype(jnp.float32)
-        ).astype(jnp.bfloat16)
+        own_part = out_ref[:, c : c + step].astype(jnp.float32)
+        out_ref[:, c : c + step] = (own_part + other_part.astype(jnp.float32)).astype(jnp.bfloat16)
 
     for copy in to_other:
         copy.wait_send()

time: 81.7 us -> 81.1 us (level)
  no operation moved by 1% of the time
where the time goes in v3:
time: 81.1 us; the launch traced here: 81 us
  Pallas kernels  78.5 us (97%)
  local copies, waits for them, and re-layouts  2.46 us (3%)
    pallas_call x1, Pallas kernels, body(): pl.pallas_call(functools.partial(kernel, seq_count, heads, lot, list_len)...  78.5 us
    unnamed x1, local copies, waits for them, and re-layouts  2.46 us

profile of v3, /device:TPU:0, one launch (start us, length us, event | category | flops | bytes accessed | tf_op | source)
XLA Modules:
  0.0 81.0 jit_solution(454156709118006074)
XLA Ops:
  0.0 78.5 %shard_map.73 = bf16[256,2560]{1,0:T(8,128)(2,1)} custom-call(bf16[256,384]{1,0:T(8,128)(2,1)} %q_ref.1, bf16[256,384]{1,0:T(8,128)(2,1)} %k_ref.1, bf16[256,384]{1,0:T(8,128)(2,1)} %v_ref.1, s32[3,4096]{1,0:T(4,128)} %perm_ref.1, s32[3,4,4]{2,1,0:T(4,128)} %pairs_ref.1, s32[3,4]{1,0:T(4,128)} %counts_ref.1, bf16[384,5120]{1,0:T(8,128)(2,1)} %w_ref.1), custom_call_target="tpu_custom_call" | custom-call | tf_op jit(solution)/shard_map/pallas_call | solution.py:474
  78.5 2.5 %copy.9 = bf16[256,2560]{1,0:T(8,128)(2,1)} copy(bf16[256,2560]{1,0:T(8,128)(2,1)} %shard_map.73) | data formatting | bytes 2621440
